TPU v7x, 32 devices: a whole 2x2x4 slice. The times are simulated.
32 devices in a mesh: dom: 8 (over z, y), group: 4 (over x, core).
Axes of the slice: x: 2, y: 2, z: 4, core: 2. Of those that a mesh axis runs over, the one named last changes fastest.
Arguments:
- features: bfloat16 [4096, 1024], P(('dom', 'group')), may hold values from -6 to 6
- out_grad: bfloat16 [4096, 1024], P(('dom', 'group')), may hold values from -0.1796875 to 0.1796875
- gcn_weight: bfloat16 [1024, 1024], replicated, may hold values from -0.1875 to 0.1875
- tile_index: int32 [32, 4], P(('dom', 'group')), may hold values from 0 to 2
- tile_edges: int32 [32, 4, 128, 128], P(('dom', 'group')), may hold values 0 or 1
- halo_rows: int32 [8, 4, 8, 32], P('dom', 'group'), may hold values from 0 to 127
- routes: int32 [4096, 2], P(('dom', 'group')), may hold values from 0 to 15, all different within a row; in each aligned block of 128 rows (0 to 127, 128 to 255, ...) at most 20 rows name the same one
- route_weight: float32 [4096, 2], P(('dom', 'group')), may hold values from 0.25 to 1
- up_weight: bfloat16 [16, 1024, 4096], P('dom', None, 'group'), may hold values from -0.1875 to 0.1875
- down_weight: bfloat16 [16, 4096, 1024], P('dom', 'group'), may hold values from -0.09375 to 0.09375
Outputs:
- node_out: bfloat16 [4096, 1024], P(('dom', 'group'))
- up_grad: bfloat16 [16, 1024, 4096], P('dom', None, 'group')
- down_grad: bfloat16 [16, 4096, 1024], P('dom', 'group')
Inputs may be any that keep to these rules, and one draw needn't show every extreme that they name: `routes`: in the rows of one partition no expert is named more than 20 times, and in every draw some partition names some expert exactly 20 times.
All inputs are finite; a program needn't handle non-finite values. No bound on the sum of `tile_edges` on one device may be relied on, other than what follows from the above.
Results may differ from a plain program's by a relative error of at most 0.0071.
Values may be sent and summed in bfloat16 or wider, within the bound.
A program may use at most 128 MiB of HBM per device.

v0:
```python
import jax
import jax.numpy as jnp
from jax import lax
from jax.sharding import PartitionSpec as P


def silu_slope(values):
    logistic = jax.nn.sigmoid(values)
    return logistic * (1.0 + values * (1.0 - logistic))


def slot_table(route_rows, expert_count, capacity):
    flat_ids = route_rows.reshape(-1)
    onehot = (flat_ids[:, None] == jnp.arange(expert_count, dtype=jnp.int32)[None, :]).astype(
        jnp.int32
    )
    before = jnp.cumsum(onehot, axis=0) - onehot
    within = jnp.sum(before * onehot, axis=1)
    target = flat_ids * capacity + within
    filler = (
        jnp.zeros((expert_count * capacity,), jnp.int32)
        .at[target]
        .set(jnp.arange(flat_ids.shape[0], dtype=jnp.int32) + 1)
    )
    return (target, filler)


def local(
    features,
    out_grad,
    gcn_weight,
    tile_index,
    tile_edges,
    halo_rows,
    routes,
    route_weight,
    up_weight,
    down_weight,
):
    dom_count = lax.axis_size("dom")
    group_count = lax.axis_size("group")
    node_count, width = features.shape
    tile_rows = tile_edges.shape[-1]
    local_tiles = tile_index.shape[0]
    border_rows = halo_rows.shape[-1]
    expert_local = up_weight.shape[0]
    expert_count = expert_local * dom_count
    top_count = routes.shape[1]
    capacity = max(2, 5 * node_count * top_count // (4 * expert_count))
    send_lists = halo_rows.reshape(-1)
    outgoing = features[send_lists].reshape(dom_count, border_rows, width)
    incoming = lax.all_to_all(outgoing, "dom", split_axis=0, concat_axis=0, tiled=True)
    sources = jnp.concatenate(
        [features, incoming.reshape(dom_count * border_rows, width)], axis=0
    ).reshape(-1, tile_rows, width)
    chosen = sources[tile_index]
    edge_values = tile_edges.astype(jnp.bfloat16)
    summed = features.reshape(local_tiles, tile_rows, width).astype(jnp.float32) + jnp.einsum(
        "tsij,tsjd->tid", edge_values, chosen, preferred_element_type=jnp.float32
    )
    degree = 1.0 + jnp.sum(tile_edges, axis=(1, 3)).astype(jnp.float32)
    aggregated = (
        (summed / jnp.sqrt(degree)[:, :, None]).reshape(node_count, width).astype(jnp.bfloat16)
    )
    preact = jnp.dot(aggregated, gcn_weight, preferred_element_type=jnp.float32)
    hidden = (features.astype(jnp.float32) + jax.nn.silu(preact)).astype(jnp.bfloat16)
    targets, fillers = slot_table(routes, expert_count, capacity)
    cotangent = (
        (route_weight[:, :, None] * out_grad[:, None, :].astype(jnp.float32))
        .astype(jnp.bfloat16)
        .reshape(-1, width)
    )
    present = (fillers > 0)[:, None]
    source_pair = jnp.maximum(fillers - 1, 0)
    nothing = jnp.zeros((), jnp.bfloat16)
    slot_shape = (dom_count, expert_local * capacity, width)
    send_hidden = jnp.where(present, hidden[source_pair // top_count], nothing).reshape(slot_shape)
    send_cot = jnp.where(present, cotangent[source_pair], nothing).reshape(slot_shape)
    mine_cot = lax.all_to_all(send_cot, "dom", split_axis=0, concat_axis=0, tiled=True)
    token_cot = lax.all_gather(mine_cot[None], "group", axis=0, tiled=True)
    mine_hidden = lax.all_to_all(send_hidden, "dom", split_axis=0, concat_axis=0, tiled=True)
    token_hidden = lax.all_gather(mine_hidden[None], "group", axis=0, tiled=True)
    sender_count = group_count * dom_count
    token_hidden = token_hidden.reshape(sender_count, expert_local, capacity, width)
    token_cot = token_cot.reshape(sender_count, expert_local, capacity, width)
    up_proj = jnp.einsum(
        "secd,edf->secf", token_hidden, up_weight, preferred_element_type=jnp.float32
    )
    active = jax.nn.silu(up_proj).astype(jnp.bfloat16)
    merged = lax.psum_scatter(
        jnp.einsum(
            "secf,efd->secd", active, down_weight, preferred_element_type=jnp.float32
        ).astype(jnp.bfloat16),
        "group",
        scatter_dimension=0,
        tiled=True,
    )
    expert_out = merged.reshape(dom_count, expert_local * capacity, width)
    returned = lax.all_to_all(expert_out, "dom", split_axis=0, concat_axis=0, tiled=True).reshape(
        expert_count * capacity, width
    )
    gathered = returned[targets].reshape(node_count, top_count, width)
    node_out = (
        hidden.astype(jnp.float32)
        + jnp.sum(route_weight[:, :, None] * gathered.astype(jnp.float32), axis=1)
    ).astype(jnp.bfloat16)
    grad_act = jnp.einsum(
        "secd,efd->secf", token_cot, down_weight, preferred_element_type=jnp.float32
    )
    grad_pre = (grad_act * silu_slope(up_proj)).astype(jnp.bfloat16)
    down_grad = jnp.einsum(
        "secf,secd->efd", active, token_cot, preferred_element_type=jnp.float32
    ).astype(jnp.bfloat16)
    up_grad = jnp.einsum(
        "secd,secf->edf", token_hidden, grad_pre, preferred_element_type=jnp.float32
    ).astype(jnp.bfloat16)
    return (node_out, up_grad, down_grad)


def solution(mesh):
    in_specs = (
        P(("dom", "group"), None),
        P(("dom", "group"), None),
        P(),
        P(("dom", "group"), None),
        P(("dom", "group"), None, None, None),
        P("dom", "group", None, None),
        P(("dom", "group"), None),
        P(("dom", "group"), None),
        P("dom", None, "group"),
        P("dom", "group", None),
    )
    out_specs = (P(("dom", "group"), None), P("dom", None, "group"), P("dom", "group", None))
    return jax.shard_map(local, mesh=mesh, in_specs=in_specs, out_specs=out_specs, check_vma=False)
```

profile of v0, /device:TPU:0, one launch (start us, length us, event | category | flops | bytes accessed | tf_op | source)
XLA Modules:
  0.0 192.9 jit_solution(4663778561806008242)
XLA Ops:
  8.2 3.3 %gather_fusion = bf16[256,1024]{1,0:T(8,128)(2,1)} fusion(bf16[128,1024]{1,0:T(8,128)(2,1)} %param.10, s32[1024]{0:T(1024)S(1)} %pad_clamp_fusion.4), kind=kCustom, calls=%fused_computation | custom fusion | bytes 1049600 | tf_op jit(solution)/shard_map/gather | solution.py:51
  11.5 7.3 %all-to-all-start = ((bf16[8,32,1024]{2,1,0:T(8,128)(2,1)}), bf16[8,32,1024]{2,1,0:T(8,128)(2,1)}, u32[]{:S(2)}, u32[]{:S(2)}) async-start(bf16[8,32,1024]{2,1,0:T(8,128)(2,1)} %bitcast.1), calls=%async_computation | async-start | bytes 1048576 | tf_op jit(solution)/shard_map/all_to_all | solution.py:52
  20.4 1.4 scatter_custom_fusion
  24.0 1.7 mul.73
  27.1 1.3 multiply_convert_fusion
  28.4 2.6 %gather_fusion.4 = bf16[320,1024]{1,0:T(8,128)(2,1)} fusion(bf16[256,1024]{1,0:T(8,128)(2,1)S(1)} %multiply_convert_fusion, s32[1024]{0:T(1024)S(1)} %get-tuple-element.16), kind=kCustom, calls=%fused_computation.4 | custom fusion | bytes 1312000 | tf_op jit(solution)/shard_map/gather | solution.py:78
  31.1 2.3 %all-to-all-done = bf16[8,32,1024]{2,1,0:T(8,128)(2,1)} async-done(((bf16[8,32,1024]{2,1,0:T(8,128)(2,1)}), bf16[8,32,1024]{2,1,0:T(8,128)(2,1)}, u32[]{:S(2)}, u32[]{:S(2)}) %all-to-all-start) | async-done | bytes 524320 | tf_op jit(solution)/shard_map/all_to_all | solution.py:52
  34.5 1.6 gather_fusion.1
  36.1 2.9 %fusion.24 = bf16[128,1024]{0,1:T(8,128)(2,1)S(1)} fusion(bf16[128,1024]{0,1:T(8,128)(2,1)} %copy.56, bf16[1024,1024]{1,0:T(8,128)(2,1)S(1)} %copy-done, bf16[4,128,1024]{2,1,0:T(8,128)(2,1)} %gather_fusion.1, f32[128]{0:T(128)S(1)} %add_sqrt_fusion, s32[1,4,128,128]{3,2,1,0:T(8,128)S(1)} %copy-done.6), kind=kOutput, calls=%fused_computation.38 | convolution fusion | flops 404160512 | bytes 3932672 | tf_op jit(solution)/shard_map/dot_general | solution.py:65
  39.1 2.6 %gather_fusion.2 = bf16[320,1024]{1,0:T(8,128)(2,1)} fusion(bf16[128,1024]{1,0:T(8,128)(2,1)S(1)} %copy.65, s32[1024]{0:T(1024)S(1)} %get-tuple-element.17), kind=kCustom, calls=%fused_computation.2 | custom fusion | bytes 1312000 | tf_op jit(solution)/shard_map/gather | solution.py:77
  41.8 1.2 broadcast_select_fusion
  43.0 21.4 %all_to_all.20 = bf16[8,40,1024]{2,1,0:T(8,128)(2,1)} all-to-all(bf16[8,40,1024]{2,1,0:T(8,128)(2,1)S(1)} %get-tuple-element.15), channel_id=1, replica_groups=mesh['dom'=8,'group'=4] {'dom'}, dimensions={0} | all-to-all | bytes 1310720 | tf_op jit(solution)/shard_map/all_to_all | solution.py:81
  64.5 20.7 %all_to_all.21 = bf16[8,40,1024]{2,1,0:T(8,128)(2,1)} all-to-all(bf16[8,40,1024]{2,1,0:T(8,128)(2,1)S(1)} %get-tuple-element.14), channel_id=1, replica_groups=mesh['dom'=8,'group'=4] {'dom'}, dimensions={0} | all-to-all | bytes 1310720 | tf_op jit(solution)/shard_map/all_to_all | solution.py:79
  85.4 3.4 %all-gather.5.cloned.1.call-done = bf16[32,40,1024]{2,1,0:T(8,128)(2,1)} async-done(((bf16[8,40,1024]{2,1,0:T(8,128)(2,1)}), bf16[32,40,1024]{2,1,0:T(8,128)(2,1)}) %all-gather.5.cloned.1.call-update) | async-done | bytes 2621456 | tf_op jit(solution)/shard_map/all_gather | solution.py:82
  88.8 3.3 %copy.66 = bf16[32,40,1024]{2,0,1:T(8,128)(2,1)S(1)} copy(bf16[32,40,1024]{2,1,0:T(8,128)(2,1)} %all-gather.5.cloned.1.call-done) | data formatting | bytes 5242880 | tf_op jit(solution)/shard_map/all_gather | solution.py:82
  92.2 1.5 copy-done.2
  93.7 2.9 %fusion.7 = f32[2,32,20,1024]{3,1,2,0:T(8,128)S(1)} fusion(bf16[32,2,20,1024]{3,0,2,1:T(8,128)(2,1)S(1)} %bitcast.122, bf16[2,1024,1024]{2,1,0:T(8,128)(2,1)S(1)} %copy-done.9), kind=kOutput, calls=%fused_computation.19 | convolution fusion | flops 2684354560 | bytes 12058624 | tf_op jit(solution)/shard_map/secd,edf->secf/dot_general | solution.py:86
  96.6 3.1 %convert_bitcast_fusion = bf16[32,2,20,1024]{3,0,2,1:T(8,128)(2,1)S(1)} fusion(bf16[2,1024,1024]{2,1,0:T(8,128)(2,1)S(1)} %copy-done.10, f32[2,32,20,1024]{3,1,2,0:T(8,128)S(1)} %fusion.7), kind=kOutput, calls=%fused_computation.25 | convolution fusion | flops 2692218880 | bytes 12058624 | tf_op jit(solution)/shard_map/secf,efd->secd/dot_general | solution.py:91
  99.8 3.1 %copy.78 = bf16[32,2,20,1024]{3,2,1,0:T(8,128)(2,1)} copy(bf16[32,2,20,1024]{3,0,2,1:T(8,128)(2,1)S(1)} %convert_bitcast_fusion) | data formatting | bytes 5242880
  102.9 4.9 %reshape.226 = bf16[32,40960]{1,0:T(8,128)(2,1)} reshape(bf16[32,2,20,1024]{3,2,1,0:T(8,128)(2,1)} %copy.78) | data formatting | bytes 5242880
  107.9 8.1 %all-gather.7.cloned.1.call-done = bf16[32,40,1024]{2,1,0:T(8,128)(2,1)} async-done(((bf16[8,40,1024]{2,1,0:T(8,128)(2,1)}), bf16[32,40,1024]{2,1,0:T(8,128)(2,1)}) %all-gather.7.cloned.1.call-update) | async-done | bytes 2621456 | tf_op jit(solution)/shard_map/all_gather | solution.py:80
  116.0 4.7 %copy.70 = bf16[32,40,1024]{2,0,1:T(8,128)(2,1)} copy(bf16[32,40,1024]{2,1,0:T(8,128)(2,1)} %all-gather.7.cloned.1.call-done) | data formatting | bytes 5242880 | tf_op jit(solution)/shard_map/all_gather | solution.py:80
  120.7 12.2 %bitcast_convert_fusion.1 = bf16[2,1024,1024]{2,1,0:T(8,128)(2,1)} fusion(bf16[32,2,20,1024]{3,0,2,1:T(8,128)(2,1)} %bitcast.123, f32[2,32,20,1024]{3,1,2,0:T(8,128)} %copy-done.12, bf16[32,2,20,1024]{3,0,2,1:T(8,128)(2,1)} %bitcast.124, bf16[2,1024,1024]{2,1,0:T(8,128)(2,1)} %param.19), kind=kOutput, calls=%fused_computation.7 | convolution fusion | flops 5382602752 | bytes 18874368 | tf_op jit(solution)/shard_map/secd,secf->edf/dot_general | solution.py:114
  132.9 20.3 %reduce-scatter.4.cloned.1.call-done = bf16[8,40960]{1,0:T(8,128)(2,1)} async-done(((bf16[32,40960]{1,0:T(8,128)(2,1)}), bf16[8,40960]{1,0:T(8,128)(2,1)}) %reduce-scatter.4.cloned.1.call-update) | async-done | bytes 655376
  153.2 2.3 %copy.67 = bf16[8,40,1024]{2,1,0:T(8,128)(2,1)} copy(bf16[8,40,1024]{2,0,1:T(8,128)(2,1)} %bitcast.128) | data formatting | bytes 1310720 | tf_op jit(solution)/shard_map/reshape | solution.py:98
  155.6 5.5 %all-to-all-start.2 = ((bf16[8,40,1024]{2,1,0:T(8,128)(2,1)}), bf16[8,40,1024]{2,1,0:T(8,128)(2,1)S(1)}, u32[]{:S(2)}, u32[]{:S(2)}) async-start(bf16[8,40,1024]{2,1,0:T(8,128)(2,1)} %copy.67), calls=%async_computation.2 | async-start | bytes 1310720 | tf_op jit(solution)/shard_map/all_to_all | solution.py:99
  161.1 8.9 %bitcast_convert_fusion = bf16[2,1024,1024]{2,1,0:T(8,128)(2,1)} fusion(bf16[32,2,20,1024]{3,0,2,1:T(8,128)(2,1)} %bitcast.125, f32[2,32,20,1024]{3,1,2,0:T(8,128)} %copy-done.12), kind=kOutput, calls=%fused_computation.6 | convolution fusion | flops 2693005312 | bytes 12058624 | tf_op jit(solution)/shard_map/secf,secd->efd/dot_general | solution.py:111
  169.9 8.4 %all-to-all-done.2 = bf16[8,40,1024]{2,1,0:T(8,128)(2,1)S(1)} async-done(((bf16[8,40,1024]{2,1,0:T(8,128)(2,1)}), bf16[8,40,1024]{2,1,0:T(8,128)(2,1)S(1)}, u32[]{:S(2)}, u32[]{:S(2)}) %all-to-all-start.2) | async-done | bytes 655392 | tf_op jit(solution)/shard_map/all_to_all | solution.py:99
  178.4 2.0 %gather_fusion.3 = bf16[256,1024]{1,0:T(8,128)(2,1)} fusion(bf16[320,1024]{1,0:T(8,128)(2,1)S(1)} %bitcast.120, s32[1024]{0:T(1024)S(1)} %pad_clamp_fusion.1), kind=kCustom, calls=%fused_computation.3 | custom fusion | bytes 1049600 | tf_op jit(solution)/shard_map/gather | solution.py:102
  180.3 1.7 reshape.164
  182.0 2.1 %multiply_reduce_fusion = f32[128,1024]{1,0:T(8,128)} fusion(f32[128,2,1024]{2,1,0:T(2,128)S(1)} %reshape.164, f32[128,2]{1,0:T(8,128)S(1)} %copy.60), kind=kLoop, calls=%fused_computation.32 | loop fusion | flops 393216 | bytes 1573888 | tf_op jit(solution)/shard_map/reduce_sum | solution.py:105
  184.2 1.2 copy.68
  (65 shorter events, 8.6 us)
Async XLA Ops:
  7.2 28.9 %copy-start = (bf16[1024,1024]{1,0:T(8,128)(2,1)S(1)}, bf16[1024,1024]{1,0:T(8,128)(2,1)}, u32[]{:S(2)}) copy-start(bf16[1024,1024]{1,0:T(8,128)(2,1)} %param.12) | copy-start | bytes 6291460
  7.2 14.7 %copy-start.1 = (bf16[128,1024]{1,0:T(8,128)(2,1)S(1)}, bf16[128,1024]{1,0:T(8,128)(2,1)}, u32[]{:S(2)}) copy-start(bf16[128,1024]{1,0:T(8,128)(2,1)} %param.10) | copy-start | bytes 786436
  7.2 11.6 %copy-start.7 = (s32[128,2]{0,1:T(2,128)S(1)}, s32[128,2]{0,1:T(2,128)}, u32[]{:S(2)}) copy-start(s32[128,2]{0,1:T(2,128)} %param.16) | copy-start | bytes 3076
  8.1 17.5 %copy-start.8 = (f32[128,2]{0,1:T(2,128)S(1)}, f32[128,2]{0,1:T(2,128)}, u32[]{:S(2)}) copy-start(f32[128,2]{0,1:T(2,128)} %param.17) | copy-start | bytes 3076
  11.5 21.9 %all-to-all-start = ((bf16[8,32,1024]{2,1,0:T(8,128)(2,1)}), bf16[8,32,1024]{2,1,0:T(8,128)(2,1)}, u32[]{:S(2)}, u32[]{:S(2)}) async-start(bf16[8,32,1024]{2,1,0:T(8,128)(2,1)} %bitcast.1), calls=%async_computation | async-start | bytes 1048576 | tf_op jit(solution)/shard_map/all_to_all | solution.py:52
  18.8 70.0 %all-gather.5.cloned.1.call-start = ((), (), s32[]{:S(2)}) async-start(), calls=%async_computation.5 | async-start | bytes 3276800 | tf_op jit(solution)/shard_map/all_gather | solution.py:82
  25.6 5.4 %copy-start.11 = (s32[1,4]{1,0:T(1,128)S(1)}, s32[1,4]{1,0:T(1,128)}, u32[]{:S(2)}) copy-start(s32[1,4]{1,0:T(1,128)} %param.13) | copy-start | bytes 52
  28.4 7.6 %copy-start.6 = (s32[1,4,128,128]{3,2,1,0:T(8,128)S(1)}, s32[1,4,128,128]{3,2,1,0:T(8,128)}, u32[]{:S(2)}) copy-start(s32[1,4,128,128]{3,2,1,0:T(8,128)} %param.14) | copy-start | bytes 786436
  38.9 2.8 %copy-start.4 = (bf16[128,1024]{0,1:T(8,128)(2,1)}, bf16[128,1024]{0,1:T(8,128)(2,1)S(1)}, u32[]{:S(2)}) copy-start(bf16[128,1024]{0,1:T(8,128)(2,1)S(1)} %fusion.24) | copy-start | bytes 786436
  38.9 2.8 %copy-start.3 = (bf16[320,1024]{1,0:T(8,128)(2,1)S(1)}, bf16[320,1024]{1,0:T(8,128)(2,1)}, u32[]{:S(2)}) copy-start(bf16[320,1024]{1,0:T(8,128)(2,1)} %gather_fusion.4) | copy-start | bytes 1966084
  64.4 51.5 %all-gather.7.cloned.1.call-start = ((), (), s32[]{:S(2)}) async-start(), calls=%async_computation.6 | async-start | bytes 3276800 | tf_op jit(solution)/shard_map/all_gather | solution.py:80
  85.2 68.0 %reduce-scatter.4.cloned.1.call-start = ((), (), s32[]{:S(2)}) async-start(), calls=%async_computation.7 | async-start | bytes 3276800
  88.8 4.9 %copy-start.9 = (bf16[2,1024,1024]{2,1,0:T(8,128)(2,1)S(1)}, bf16[2,1024,1024]{2,1,0:T(8,128)(2,1)}, u32[]{:S(2)}) copy-start(bf16[2,1024,1024]{2,1,0:T(8,128)(2,1)} %param.18) | copy-start | bytes 12582916
  92.1 1.5 copy-start.2
  93.7 2.9 %copy-start.10 = (bf16[2,1024,1024]{2,1,0:T(8,128)(2,1)S(1)}, bf16[2,1024,1024]{2,1,0:T(8,128)(2,1)}, u32[]{:S(2)}) copy-start(bf16[2,1024,1024]{2,1,0:T(8,128)(2,1)} %param.19) | copy-start | bytes 12582916
  96.6 3.2 %copy-start.12 = (f32[2,32,20,1024]{3,1,2,0:T(8,128)}, f32[2,32,20,1024]{3,1,2,0:T(8,128)S(1)}, u32[]{:S(2)}) copy-start(f32[2,32,20,1024]{3,1,2,0:T(8,128)S(1)} %fusion.7) | copy-start | bytes 15728644
  155.6 22.8 %all-to-all-start.2 = ((bf16[8,40,1024]{2,1,0:T(8,128)(2,1)}), bf16[8,40,1024]{2,1,0:T(8,128)(2,1)S(1)}, u32[]{:S(2)}, u32[]{:S(2)}) async-start(bf16[8,40,1024]{2,1,0:T(8,128)(2,1)} %copy.67), calls=%async_computation.2 | async-start | bytes 1310720 | tf_op jit(solution)/shard_map/all_to_all | solution.py:99
  178.4 7.0 %copy-start.5 = (bf16[128,1024]{0,1:T(8,128)(2,1)S(1)}, bf16[128,1024]{0,1:T(8,128)(2,1)}, u32[]{:S(2)}) copy-start(bf16[128,1024]{0,1:T(8,128)(2,1)} %copy-done.4) | copy-start | bytes 786436
Sparse Core Ops, SparseCore 0:
  64.5 24.2 all-gather.4
  90.4 25.5 all-gather.6
  118.5 34.6 reduce-scatter.3
where the time goes:
time: 194 us; the launch traced here: 193 us
  local copies, waits for them, and re-layouts  43.4 us (22%)
  waiting for transfers between devices  42.6 us (22%)
  blocking collectives  42.1 us (22%)
  matrix products  30 us (15%)
  between operations  14 us (7%)
  starting transfers between devices  13.1 us (7%)
  other arithmetic  7.74 us (4%)
    all_to_all x1, blocking collectives, local(): lax.all_to_all(send_hidden, 'dom', split_axis=0, concat_axis=0, tiled=True)  21.4 us
    all_to_all x1, blocking collectives, local(): lax.all_to_all(send_cot, 'dom', split_axis=0, concat_axis=0, tiled=True)  20.7 us
    unnamed x4, waiting for transfers between devices  20.4 us
    dot_general x1, matrix products, local(): jnp.einsum('secd,secf->edf', token_hidden, grad_pre, preferred_element_ty...  12.2 us
    unnamed x32, local copies, waits for them, and re-layouts  11.6 us
    dot_general x1, matrix products, local(): jnp.einsum('secf,secd->efd', active, token_cot, preferred_element_type=jn...  8.86 us
    all_to_all x1, waiting for transfers between devices, local(): lax.all_to_all(expert_out, 'dom', split_axis=0, concat_axis=0, tiled=True)  8.44 us
    all_gather x1, waiting for transfers between devices, local(): token_cot = lax.all_gather(mine_cot[None], 'group', axis=0, tiled=True)  8.1 us
  transfers between devices with their start and end apart: 5, of which 5 were waited for; matrix products, arithmetic and copies ran while one was open for 29% of the time, Pallas kernels for 0%

commit v1 on v0

--- a/solution.py
+++ b/solution.py
@@ -78,7 +78,15 @@
     send_cot = jnp.where(present, cotangent[source_pair], nothing).reshape(slot_shape)
     mine_cot = lax.all_to_all(send_cot, "dom", split_axis=0, concat_axis=0, tiled=True)
     token_cot = lax.all_gather(mine_cot[None], "group", axis=0, tiled=True)
-    mine_hidden = lax.all_to_all(send_hidden, "dom", split_axis=0, concat_axis=0, tiled=True)
+    ways, here = (lax.axis_size("dom"), lax.axis_index("dom"))
+    width_2 = send_hidden.shape[0] // ways
+    turned = jnp.roll(send_hidden, -here * width_2, axis=0)
+    got = [lax.slice_in_dim(turned, 0, width_2, axis=0)]
+    for far in range(1, ways):
+        sent = lax.slice_in_dim(turned, far * width_2, (far + 1) * width_2, axis=0)
+        got.append(lax.ppermute(sent, "dom", [(d, (d + far) % ways) for d in range(ways)]))
+    line = jnp.concatenate(got[::-1], axis=0)
+    mine_hidden = jnp.roll(line, (here + 1) * got[0].shape[0], axis=0)
     token_hidden = lax.all_gather(mine_hidden[None], "group", axis=0, tiled=True)
     sender_count = group_count * dom_count
     token_hidden = token_hidden.reshape(sender_count, expert_local, capacity, width)

time: 194 us -> 196 us (1.010)
  blocking collectives: 42.1 us -> 20 us
  waiting for transfers between devices: 42.6 us -> 53.3 us
  starting transfers between devices: 13.1 us -> 21.9 us
  other arithmetic: 7.74 us -> 10.1 us
  local copies, waits for them, and re-layouts: 43.4 us -> 45.5 us
    all_to_all x1 -> x0, blocking collectives: 21.4 us -> none  [local(): lax.all_to_all(send_hidden, 'dom', split_axis=0, concat_axis=0, tiled=True)]
    ppermute x0 -> x7, waiting for transfers between devices: none -> 9.51 us  [local(): lax.ppermute(sent, 'dom', [(d, (d + far) % ways) for d in range(ways)])]
    ppermute x0 -> x7, starting transfers between devices: none -> 8.83 us  [local(): lax.ppermute(sent, 'dom', [(d, (d + far) % ways) for d in range(ways)])]
    unnamed x32 -> x39, local copies, waits for them, and re-layouts: 11.6 us -> 13.2 us
  transfers between devices with their start and end apart: 5 -> 12, of which waited for: 5 -> 7; matrix products, arithmetic and copies ran while one was open for 29% -> 28% of each run, Pallas kernels for 0% -> 0%
where the time goes in v1:
time: 196 us; the launch traced here: 195 us
  waiting for transfers between devices  53.3 us (27%)
  local copies, waits for them, and re-layouts  45.5 us (23%)
  matrix products  30 us (15%)
  starting transfers between devices  21.9 us (11%)
  blocking collectives  20 us (10%)
  between operations  14.1 us (7%)
  other arithmetic  10.1 us (5%)
    unnamed x4, waiting for transfers between devices  20.4 us
    all_to_all x1, blocking collectives, local(): lax.all_to_all(send_cot, 'dom', split_axis=0, concat_axis=0, tiled=True)  20 us
    unnamed x39, local copies, waits for them, and re-layouts  13.2 us
    dot_general x1, matrix products, local(): jnp.einsum('secd,secf->edf', token_hidden, grad_pre, preferred_element_ty...  12.2 us
    ppermute x7, waiting for transfers between devices, local(): lax.ppermute(sent, 'dom', [(d, (d + far) % ways) for d in range(ways)])  9.51 us
    dot_general x1, matrix products, local(): jnp.einsum('secf,secd->efd', active, token_cot, preferred_element_type=jn...  8.86 us
    ppermute x7, starting transfers between devices, local(): lax.ppermute(sent, 'dom', [(d, (d + far) % ways) for d in range(ways)])  8.83 us
    all_to_all x1, waiting for transfers between devices, local(): lax.all_to_all(expert_out, 'dom', split_axis=0, concat_axis=0, tiled=True)  8.44 us
  transfers between devices with their start and end apart: 12, of which 7 were waited for; matrix products, arithmetic and copies ran while one was open for 28% of the time, Pallas kernels for 0%

profile of v1, /device:TPU:0, one launch (start us, length us, event | category | flops | bytes accessed | tf_op | source)
XLA Modules:
  0.0 194.9 jit_solution(16307374909151946737)
XLA Ops:
  11.1 3.3 %gather_fusion = bf16[256,1024]{1,0:T(8,128)(2,1)} fusion(bf16[128,1024]{1,0:T(8,128)(2,1)} %param.12, s32[1024]{0:T(1024)S(1)} %pad_clamp_fusion.4), kind=kCustom, calls=%fused_computation | custom fusion | bytes 1049600 | tf_op jit(solution)/shard_map/gather | solution.py:51
  14.4 7.3 %all-to-all-start = ((bf16[8,32,1024]{2,1,0:T(8,128)(2,1)}), bf16[8,32,1024]{2,1,0:T(8,128)(2,1)}, u32[]{:S(2)}, u32[]{:S(2)}) async-start(bf16[8,32,1024]{2,1,0:T(8,128)(2,1)} %bitcast.1), calls=%async_computation | async-start | bytes 1048576 | tf_op jit(solution)/shard_map/all_to_all | solution.py:52
  25.3 1.7 mul.73
  29.8 2.6 %gather_fusion.4 = bf16[320,1024]{1,0:T(8,128)(2,1)} fusion(bf16[256,1024]{1,0:T(8,128)(2,1)S(1)} %multiply_convert_fusion, s32[1024]{0:T(1024)S(1)} %pad_clamp_fusion), kind=kCustom, calls=%fused_computation.4 | custom fusion | bytes 1312000 | tf_op jit(solution)/shard_map/gather | solution.py:78
  32.5 3.8 %all-to-all-done = bf16[8,32,1024]{2,1,0:T(8,128)(2,1)} async-done(((bf16[8,32,1024]{2,1,0:T(8,128)(2,1)}), bf16[8,32,1024]{2,1,0:T(8,128)(2,1)}, u32[]{:S(2)}, u32[]{:S(2)}) %all-to-all-start) | async-done | bytes 524320 | tf_op jit(solution)/shard_map/all_to_all | solution.py:52
  37.4 1.6 gather_fusion.1
  39.0 2.9 %fusion.26 = bf16[128,1024]{0,1:T(8,128)(2,1)S(1)} fusion(bf16[128,1024]{0,1:T(8,128)(2,1)} %copy.56, bf16[1024,1024]{1,0:T(8,128)(2,1)S(1)} %copy-done, bf16[4,128,1024]{2,1,0:T(8,128)(2,1)} %gather_fusion.1, f32[128]{0:T(128)S(1)} %add_sqrt_fusion, s32[1,4,128,128]{3,2,1,0:T(8,128)S(1)} %copy-done.5), kind=kOutput, calls=%fused_computation.44 | convolution fusion | flops 404160512 | bytes 3932672 | tf_op jit(solution)/shard_map/dot_general | solution.py:65
  42.0 2.6 %gather_fusion.2 = bf16[320,1024]{1,0:T(8,128)(2,1)} fusion(bf16[128,1024]{1,0:T(8,128)(2,1)S(1)} %copy.65, s32[1024]{0:T(1024)S(1)} %pad_clamp_fusion.2), kind=kCustom, calls=%fused_computation.2 | custom fusion | bytes 1312000 | tf_op jit(solution)/shard_map/gather | solution.py:77
  47.2 2.4 %collective-permute-start = (bf16[1,40,1024]{2,1,0:T(8,128)(2,1)}, bf16[1,40,1024]{2,1,0:T(8,128)(2,1)}, u32[]{:S(2)}, u32[]{:S(2)}) collective-permute-start(bf16[1,40,1024]{2,1,0:T(8,128)(2,1)} %get-tuple-element.19), channel_id=1, source_target_pairs={{0,28},{4,0},{8,4},{12,8},{16,12},{20,16},{24,20},{28,24},{1,29},{... | collective-permute-start | bytes 245768 | tf_op jit(solution)/shard_map/ppermute | solution.py:87
  50.9 1.9 collective-permute-start.3
  52.7 1.7 collective-permute-start.4
  56.9 7.0 %collective-permute-done.3 = bf16[1,40,1024]{2,1,0:T(8,128)(2,1)S(1)} collective-permute-done((bf16[1,40,1024]{2,1,0:T(8,128)(2,1)}, bf16[1,40,1024]{2,1,0:T(8,128)(2,1)S(1)}, u32[]{:S(2)}, u32[]{:S(2)}) %collective-permute-start.3) | collective-permute-done | bytes 81952 | tf_op jit(solution)/shard_map/ppermute | solution.py:87
  63.9 2.5 %collective-permute-done.4 = bf16[1,40,1024]{2,1,0:T(8,128)(2,1)S(1)} collective-permute-done((bf16[1,40,1024]{2,1,0:T(8,128)(2,1)}, bf16[1,40,1024]{2,1,0:T(8,128)(2,1)S(1)}, u32[]{:S(2)}, u32[]{:S(2)}) %collective-permute-start.4) | collective-permute-done | bytes 81952 | tf_op jit(solution)/shard_map/ppermute | solution.py:87
  67.7 20.0 %all_to_all.15 = bf16[8,40,1024]{2,1,0:T(8,128)(2,1)} all-to-all(bf16[8,40,1024]{2,1,0:T(8,128)(2,1)S(1)} %get-tuple-element.22), channel_id=1, replica_groups=mesh['dom'=8,'group'=4] {'dom'}, dimensions={0} | all-to-all | bytes 1310720 | tf_op jit(solution)/shard_map/all_to_all | solution.py:79
  87.9 3.0 %all-gather.5.cloned.1.call-done = bf16[32,40,1024]{2,1,0:T(8,128)(2,1)} async-done(((bf16[8,40,1024]{2,1,0:T(8,128)(2,1)}), bf16[32,40,1024]{2,1,0:T(8,128)(2,1)}) %all-gather.5.cloned.1.call-update) | async-done | bytes 2621456 | tf_op jit(solution)/shard_map/all_gather | solution.py:90
  90.9 3.3 %copy.66 = bf16[32,40,1024]{2,0,1:T(8,128)(2,1)S(1)} copy(bf16[32,40,1024]{2,1,0:T(8,128)(2,1)} %all-gather.5.cloned.1.call-done) | data formatting | bytes 5242880 | tf_op jit(solution)/shard_map/all_gather | solution.py:90
  94.2 1.6 copy-done.2
  95.8 2.9 %fusion.7 = f32[2,32,20,1024]{3,1,2,0:T(8,128)S(1)} fusion(bf16[32,2,20,1024]{3,0,2,1:T(8,128)(2,1)S(1)} %bitcast.122, bf16[2,1024,1024]{2,1,0:T(8,128)(2,1)S(1)} %copy-done.9), kind=kOutput, calls=%fused_computation.19 | convolution fusion | flops 2684354560 | bytes 12058624 | tf_op jit(solution)/shard_map/secd,edf->secf/dot_general | solution.py:94
  98.7 3.1 %convert_bitcast_fusion = bf16[32,2,20,1024]{3,0,2,1:T(8,128)(2,1)S(1)} fusion(bf16[2,1024,1024]{2,1,0:T(8,128)(2,1)S(1)} %copy-done.10, f32[2,32,20,1024]{3,1,2,0:T(8,128)S(1)} %fusion.7), kind=kOutput, calls=%fused_computation.25 | convolution fusion | flops 2692218880 | bytes 12058624 | tf_op jit(solution)/shard_map/secf,efd->secd/dot_general | solution.py:99
  101.9 3.1 %copy.78 = bf16[32,2,20,1024]{3,2,1,0:T(8,128)(2,1)} copy(bf16[32,2,20,1024]{3,0,2,1:T(8,128)(2,1)S(1)} %convert_bitcast_fusion) | data formatting | bytes 5242880
  105.0 4.9 %reshape.226 = bf16[32,40960]{1,0:T(8,128)(2,1)} reshape(bf16[32,2,20,1024]{3,2,1,0:T(8,128)(2,1)} %copy.78) | data formatting | bytes 5242880
  109.9 8.1 %all-gather.7.cloned.1.call-done = bf16[32,40,1024]{2,1,0:T(8,128)(2,1)} async-done(((bf16[8,40,1024]{2,1,0:T(8,128)(2,1)}), bf16[32,40,1024]{2,1,0:T(8,128)(2,1)}) %all-gather.7.cloned.1.call-update) | async-done | bytes 2621456 | tf_op jit(solution)/shard_map/all_gather | solution.py:80
  118.0 4.6 %copy.70 = bf16[32,40,1024]{2,0,1:T(8,128)(2,1)} copy(bf16[32,40,1024]{2,1,0:T(8,128)(2,1)} %all-gather.7.cloned.1.call-done) | data formatting | bytes 5242880 | tf_op jit(solution)/shard_map/all_gather | solution.py:80
  122.7 12.2 %bitcast_convert_fusion.1 = bf16[2,1024,1024]{2,1,0:T(8,128)(2,1)} fusion(bf16[32,2,20,1024]{3,0,2,1:T(8,128)(2,1)} %bitcast.123, f32[2,32,20,1024]{3,1,2,0:T(8,128)} %copy-done.12, bf16[32,2,20,1024]{3,0,2,1:T(8,128)(2,1)} %bitcast.124, bf16[2,1024,1024]{2,1,0:T(8,128)(2,1)} %param.21), kind=kOutput, calls=%fused_computation.7 | convolution fusion | flops 5382602752 | bytes 18874368 | tf_op jit(solution)/shard_map/secd,secf->edf/dot_general | solution.py:122
  134.9 20.4 %reduce-scatter.4.cloned.1.call-done = bf16[8,40960]{1,0:T(8,128)(2,1)} async-done(((bf16[32,40960]{1,0:T(8,128)(2,1)}), bf16[8,40960]{1,0:T(8,128)(2,1)}) %reduce-scatter.4.cloned.1.call-update) | async-done | bytes 655376
  155.3 2.3 %copy.67 = bf16[8,40,1024]{2,1,0:T(8,128)(2,1)} copy(bf16[8,40,1024]{2,0,1:T(8,128)(2,1)} %bitcast.128) | data formatting | bytes 1310720 | tf_op jit(solution)/shard_map/reshape | solution.py:106
  157.6 5.5 %all-to-all-start.1 = ((bf16[8,40,1024]{2,1,0:T(8,128)(2,1)}), bf16[8,40,1024]{2,1,0:T(8,128)(2,1)S(1)}, u32[]{:S(2)}, u32[]{:S(2)}) async-start(bf16[8,40,1024]{2,1,0:T(8,128)(2,1)} %copy.67), calls=%async_computation.1 | async-start | bytes 1310720 | tf_op jit(solution)/shard_map/all_to_all | solution.py:107
  163.1 8.9 %bitcast_convert_fusion = bf16[2,1024,1024]{2,1,0:T(8,128)(2,1)} fusion(bf16[32,2,20,1024]{3,0,2,1:T(8,128)(2,1)} %bitcast.125, f32[2,32,20,1024]{3,1,2,0:T(8,128)} %copy-done.12), kind=kOutput, calls=%fused_computation.6 | convolution fusion | flops 2693005312 | bytes 12058624 | tf_op jit(solution)/shard_map/secf,secd->efd/dot_general | solution.py:119
  172.0 8.4 %all-to-all-done.1 = bf16[8,40,1024]{2,1,0:T(8,128)(2,1)S(1)} async-done(((bf16[8,40,1024]{2,1,0:T(8,128)(2,1)}), bf16[8,40,1024]{2,1,0:T(8,128)(2,1)S(1)}, u32[]{:S(2)}, u32[]{:S(2)}) %all-to-all-start.1) | async-done | bytes 655392 | tf_op jit(solution)/shard_map/all_to_all | solution.py:107
  180.4 2.0 %gather_fusion.3 = bf16[256,1024]{1,0:T(8,128)(2,1)} fusion(bf16[320,1024]{1,0:T(8,128)(2,1)S(1)} %bitcast.120, s32[1024]{0:T(1024)S(1)} %pad_clamp_fusion.1), kind=kCustom, calls=%fused_computation.3 | custom fusion | bytes 1049600 | tf_op jit(solution)/shard_map/gather | solution.py:110
  182.4 1.7 reshape.164
  184.1 2.1 %multiply_reduce_fusion = f32[128,1024]{1,0:T(8,128)} fusion(f32[128,2,1024]{2,1,0:T(2,128)S(1)} %reshape.164, f32[128,2]{1,0:T(8,128)S(1)} %copy.60), kind=kLoop, calls=%fused_computation.36 | loop fusion | flops 393216 | bytes 1573888 | tf_op jit(solution)/shard_map/reduce_sum | solution.py:113
  (89 shorter events, 21.2 us)
Async XLA Ops:
  7.2 31.8 %copy-start = (bf16[1024,1024]{1,0:T(8,128)(2,1)S(1)}, bf16[1024,1024]{1,0:T(8,128)(2,1)}, u32[]{:S(2)}) copy-start(bf16[1024,1024]{1,0:T(8,128)(2,1)} %param.14) | copy-start | bytes 6291460
  7.2 16.0 %copy-start.1 = (bf16[128,1024]{1,0:T(8,128)(2,1)S(1)}, bf16[128,1024]{1,0:T(8,128)(2,1)}, u32[]{:S(2)}) copy-start(bf16[128,1024]{1,0:T(8,128)(2,1)} %param.12) | copy-start | bytes 786436
  11.1 13.0 %copy-start.6 = (s32[256,1]{0,1:T(1,128)}, s32[256,1]{0,1:T(1,128)S(1)}, u32[]{:S(2)}) copy-start(s32[256,1]{0,1:T(1,128)S(1)} %get-tuple-element.24) | copy-start | bytes 3076
  11.1 15.9 %copy-start.8 = (f32[128,2]{0,1:T(2,128)S(1)}, f32[128,2]{0,1:T(2,128)}, u32[]{:S(2)}) copy-start(f32[128,2]{0,1:T(2,128)} %param.19) | copy-start | bytes 3076
  14.4 21.9 %all-to-all-start = ((bf16[8,32,1024]{2,1,0:T(8,128)(2,1)}), bf16[8,32,1024]{2,1,0:T(8,128)(2,1)}, u32[]{:S(2)}, u32[]{:S(2)}) async-start(bf16[8,32,1024]{2,1,0:T(8,128)(2,1)} %bitcast.1), calls=%async_computation | async-start | bytes 1048576 | tf_op jit(solution)/shard_map/all_to_all | solution.py:52
  21.7 69.2 %all-gather.5.cloned.1.call-start = ((), (), s32[]{:S(2)}) async-start(), calls=%async_computation.4 | async-start | bytes 3276800 | tf_op jit(solution)/shard_map/all_gather | solution.py:90
  27.0 5.4 %copy-start.11 = (s32[1,4]{1,0:T(1,128)S(1)}, s32[1,4]{1,0:T(1,128)}, u32[]{:S(2)}) copy-start(s32[1,4]{1,0:T(1,128)} %param.15) | copy-start | bytes 52
  29.8 9.2 %copy-start.5 = (s32[1,4,128,128]{3,2,1,0:T(8,128)S(1)}, s32[1,4,128,128]{3,2,1,0:T(8,128)}, u32[]{:S(2)}) copy-start(s32[1,4,128,128]{3,2,1,0:T(8,128)} %param.16) | copy-start | bytes 786436
  41.9 4.3 %copy-start.3 = (bf16[128,1024]{0,1:T(8,128)(2,1)}, bf16[128,1024]{0,1:T(8,128)(2,1)S(1)}, u32[]{:S(2)}) copy-start(bf16[128,1024]{0,1:T(8,128)(2,1)S(1)} %fusion.26) | copy-start | bytes 786436
  47.2 7.3 %collective-permute-start = (bf16[1,40,1024]{2,1,0:T(8,128)(2,1)}, bf16[1,40,1024]{2,1,0:T(8,128)(2,1)}, u32[]{:S(2)}, u32[]{:S(2)}) collective-permute-start(bf16[1,40,1024]{2,1,0:T(8,128)(2,1)} %get-tuple-element.19), channel_id=1, source_target_pairs={{0,28},{4,0},{8,4},{12,8},{16,12},{20,16},{24,20},{28,24},{1,29},{... | collective-permute-start | bytes 245768 | tf_op jit(solution)/shard_map/ppermute | solution.py:87
  49.5 5.9 %collective-permute-start.1 = (bf16[1,40,1024]{2,1,0:T(8,128)(2,1)}, bf16[1,40,1024]{2,1,0:T(8,128)(2,1)S(1)}, u32[]{:S(2)}, u32[]{:S(2)}) collective-permute-start(bf16[1,40,1024]{2,1,0:T(8,128)(2,1)} %get-tuple-element.18), channel_id=1, source_target_pairs={{0,24},{4,28},{8,0},{12,4},{16,8},{20,12},{24,16},{28,20},{1,25},{... | collective-permute-start | bytes 245768 | tf_op jit(solution)/shard_map/ppermute | solution.py:87
  49.5 7.4 %collective-permute-start.2 = (bf16[1,40,1024]{2,1,0:T(8,128)(2,1)}, bf16[1,40,1024]{2,1,0:T(8,128)(2,1)S(1)}, u32[]{:S(2)}, u32[]{:S(2)}) collective-permute-start(bf16[1,40,1024]{2,1,0:T(8,128)(2,1)} %get-tuple-element.17), channel_id=1, source_target_pairs={{0,20},{4,24},{8,28},{12,0},{16,4},{20,8},{24,12},{28,16},{1,21},{... | collective-permute-start | bytes 245768 | tf_op jit(solution)/shard_map/ppermute | solution.py:87
  50.9 13.1 %collective-permute-start.3 = (bf16[1,40,1024]{2,1,0:T(8,128)(2,1)}, bf16[1,40,1024]{2,1,0:T(8,128)(2,1)S(1)}, u32[]{:S(2)}, u32[]{:S(2)}) collective-permute-start(bf16[1,40,1024]{2,1,0:T(8,128)(2,1)} %get-tuple-element.16), channel_id=1, source_target_pairs={{0,16},{4,20},{8,24},{12,28},{16,0},{20,4},{24,8},{28,12},{1,17},{... | collective-permute-start | bytes 245768 | tf_op jit(solution)/shard_map/ppermute | solution.py:87
  52.7 13.7 %collective-permute-start.4 = (bf16[1,40,1024]{2,1,0:T(8,128)(2,1)}, bf16[1,40,1024]{2,1,0:T(8,128)(2,1)S(1)}, u32[]{:S(2)}, u32[]{:S(2)}) collective-permute-start(bf16[1,40,1024]{2,1,0:T(8,128)(2,1)} %get-tuple-element.15), channel_id=1, source_target_pairs={{0,12},{4,16},{8,20},{12,24},{16,28},{20,0},{24,4},{28,8},{1,13},{... | collective-permute-start | bytes 245768 | tf_op jit(solution)/shard_map/ppermute | solution.py:87
  54.5 12.0 %collective-permute-start.5 = (bf16[1,40,1024]{2,1,0:T(8,128)(2,1)}, bf16[1,40,1024]{2,1,0:T(8,128)(2,1)S(1)}, u32[]{:S(2)}, u32[]{:S(2)}) collective-permute-start(bf16[1,40,1024]{2,1,0:T(8,128)(2,1)} %get-tuple-element.14), channel_id=1, source_target_pairs={{0,8},{4,12},{8,16},{12,20},{16,24},{20,28},{24,0},{28,4},{1,9},{5... | collective-permute-start | bytes 245768 | tf_op jit(solution)/shard_map/ppermute | solution.py:87
  55.4 11.1 %collective-permute-start.6 = (bf16[1,40,1024]{2,1,0:T(8,128)(2,1)S(1)}, bf16[1,40,1024]{2,1,0:T(8,128)(2,1)S(1)}, u32[]{:S(2)}, u32[]{:S(2)}) collective-permute-start(bf16[1,40,1024]{2,1,0:T(8,128)(2,1)S(1)} %get-tuple-element.13), channel_id=1, source_target_pairs={{0,4},{4,8},{8,12},{12,16},{16,20},{20,24},{24,28},{28,0},{1,5},{5... | collective-permute-start | bytes 245768 | tf_op jit(solution)/shard_map/ppermute | solution.py:87
  67.6 50.4 %all-gather.7.cloned.1.call-start = ((), (), s32[]{:S(2)}) async-start(), calls=%async_computation.5 | async-start | bytes 3276800 | tf_op jit(solution)/shard_map/all_gather | solution.py:80
  87.7 67.6 %reduce-scatter.4.cloned.1.call-start = ((), (), s32[]{:S(2)}) async-start(), calls=%async_computation.6 | async-start | bytes 3276800
  90.9 4.9 %copy-start.9 = (bf16[2,1024,1024]{2,1,0:T(8,128)(2,1)S(1)}, bf16[2,1024,1024]{2,1,0:T(8,128)(2,1)}, u32[]{:S(2)}) copy-start(bf16[2,1024,1024]{2,1,0:T(8,128)(2,1)} %param.20) | copy-start | bytes 12582916
  94.2 1.6 copy-start.2
  95.8 2.9 %copy-start.10 = (bf16[2,1024,1024]{2,1,0:T(8,128)(2,1)S(1)}, bf16[2,1024,1024]{2,1,0:T(8,128)(2,1)}, u32[]{:S(2)}) copy-start(bf16[2,1024,1024]{2,1,0:T(8,128)(2,1)} %param.21) | copy-start | bytes 12582916
  98.7 3.2 %copy-start.12 = (f32[2,32,20,1024]{3,1,2,0:T(8,128)}, f32[2,32,20,1024]{3,1,2,0:T(8,128)S(1)}, u32[]{:S(2)}) copy-start(f32[2,32,20,1024]{3,1,2,0:T(8,128)S(1)} %fusion.7) | copy-start | bytes 15728644
  105.0 4.9 %copy-start.7 = (s32[256,1]{0,1:T(1,128)S(1)}, s32[256,1]{0,1:T(1,128)}, u32[]{:S(2)}) copy-start(s32[256,1]{0,1:T(1,128)} %copy-done.6) | copy-start | bytes 3076
  157.6 22.8 %all-to-all-start.1 = ((bf16[8,40,1024]{2,1,0:T(8,128)(2,1)}), bf16[8,40,1024]{2,1,0:T(8,128)(2,1)S(1)}, u32[]{:S(2)}, u32[]{:S(2)}) async-start(bf16[8,40,1024]{2,1,0:T(8,128)(2,1)} %copy.67), calls=%async_computation.1 | async-start | bytes 1310720 | tf_op jit(solution)/shard_map/all_to_all | solution.py:107
  180.4 7.0 %copy-start.4 = (bf16[128,1024]{0,1:T(8,128)(2,1)S(1)}, bf16[128,1024]{0,1:T(8,128)(2,1)}, u32[]{:S(2)}) copy-start(bf16[128,1024]{0,1:T(8,128)(2,1)} %copy-done.3) | copy-start | bytes 786436
Sparse Core Ops, SparseCore 0:
  67.7 23.1 all-gather.4
  92.5 25.5 all-gather.6
  120.6 34.6 reduce-scatter.3
